TPU v7x, 32 devices: a whole 2x2x4 slice. The times are simulated.
32 devices in a mesh: isl: 4 (over x, core), fsdp: 8 (over z, y).
Axes of the slice: x: 2, y: 2, z: 4, core: 2. Of those that a mesh axis runs over, the one named last changes fastest.
Arguments:
- weights: float32 [3, 7168, 4096], P(None, 'fsdp', 'isl'), may hold values from -6 to 6
- momentum: float32 [3, 7168, 4096], P(None, 'fsdp', 'isl'), may hold values from -0.12 to 0.12
- first_moment: bfloat16 [4, 3, 7168, 4096], P('isl', None, 'fsdp'), may hold values from -0.00029945374 to 0.00029945374
- second_moment: bfloat16 [4, 3, 7168, 4096], P('isl', None, 'fsdp'), may hold values from 9.95351e-09 to 9.953976e-06
- inputs: bfloat16 [2, 256, 4096], P(None, ('isl', 'fsdp')), may hold values from -6 to 6
- targets: bfloat16 [2, 256, 4096], P(None, ('isl', 'fsdp')), may hold values from -6 to 6
- overflow_step: int32 [4, 8], P('isl', 'fsdp'), may hold values from 0 to 15
Outputs:
- new_weights: float32 [3, 7168, 4096], P(None, 'fsdp', 'isl')
- new_momentum: float32 [3, 7168, 4096], P(None, 'fsdp', 'isl')
Inputs may be any that keep to these rules, and one draw needn't show every extreme that they name: `overflow_step`: A device reports an overflow at inner step k when its value equals k; values of 2 or more report none.
All inputs are finite; a program needn't handle non-finite values.
Results may differ from a plain program's by a relative error of at most 0.004.
Values may be sent and summed in bfloat16 or wider, within the bound.
A program may use at most 320 MiB of HBM per device.

v0:
```python
import math
import jax
import jax.numpy as jnp
from jax import lax
from jax.sharding import PartitionSpec as P

D = 4096
FF = 7168
inner_rate = 0.02
beta_first = 0.9
beta_second = 0.95
epsilon = 1e-08
decay_rate = 0.1
outer_rate = 0.7
nesterov_coef = 0.9


def silu_parts(preact):
    sigmoid_value = jax.nn.sigmoid(preact)
    return (preact * sigmoid_value, sigmoid_value * (1.0 + preact * (1.0 - sigmoid_value)))


def contract_last(left_side, right_side):
    return lax.dot_general(
        left_side, right_side, (((1,), (1,)), ((), ())), preferred_element_type=jnp.float32
    )


def contract_first(left_side, right_side):
    return lax.dot_general(
        left_side, right_side, (((0,), (0,)), ((), ())), preferred_element_type=jnp.float32
    )


def body(weights, momentum, first_moment, second_moment, inputs, targets, overflow_step):
    island_count = lax.axis_size("isl")
    gathered = lax.all_gather(weights.astype(jnp.bfloat16), "isl", axis=2, tiled=True).astype(
        weights.dtype
    )
    current = gathered
    moment_one = first_moment[0].astype(jnp.float32)
    moment_two = second_moment[0].astype(jnp.float32)
    inner_count = inputs.shape[0]
    island_tokens = inputs.shape[1] * lax.axis_size("fsdp")
    for inner_step in range(inner_count):
        rounded = current.astype(jnp.bfloat16)
        local_inputs = inputs[inner_step]
        local_targets = targets[inner_step]
        every_input = lax.all_gather(local_inputs, "fsdp", axis=0, tiled=True)
        gate_pre = contract_last(every_input, rounded[0]) / math.sqrt(D)
        up_pre = contract_last(every_input, rounded[1]) / math.sqrt(D)
        activated, slope = silu_parts(gate_pre)
        hidden = (activated * up_pre).astype(jnp.bfloat16)
        partial_value = jnp.dot(hidden, rounded[2], preferred_element_type=jnp.float32)
        summed = lax.psum_scatter(partial_value, "fsdp", scatter_dimension=0, tiled=True)
        outputs = local_inputs.astype(jnp.float32) + summed / math.sqrt(FF)
        own_slopes = ((outputs - local_targets.astype(jnp.float32)) / island_tokens).astype(
            jnp.bfloat16
        )
        slopes = lax.all_gather(own_slopes, "fsdp", axis=0, tiled=True)
        hidden_slope = contract_last(slopes, rounded[2]) / math.sqrt(FF)
        gate_slope = (hidden_slope * up_pre * slope).astype(jnp.bfloat16)
        up_slope = (hidden_slope * activated).astype(jnp.bfloat16)
        grad_gate = contract_first(gate_slope, every_input) / math.sqrt(D)
        grad_up = contract_first(up_slope, every_input) / math.sqrt(D)
        grad_down = contract_first(hidden, slopes) / math.sqrt(FF)
        gradient = jnp.stack([grad_gate, grad_up, grad_down])
        overflow_count = lax.psum(jnp.sum((overflow_step == inner_step).astype(jnp.int32)), "fsdp")
        skipped = overflow_count > 0
        next_one = beta_first * moment_one + (1.0 - beta_first) * gradient
        next_two = beta_second * moment_two + (1.0 - beta_second) * gradient * gradient
        next_weights = current - inner_rate * (
            next_one / (jnp.sqrt(next_two) + epsilon) + decay_rate * current
        )
        current = jnp.where(skipped, current, next_weights)
        moment_one = jnp.where(skipped, moment_one, next_one)
        moment_two = jnp.where(skipped, moment_two, next_two)
    pseudo_term = gathered - current
    pseudo_sum = lax.psum_scatter(
        pseudo_term.astype(jnp.bfloat16), "isl", scatter_dimension=2, tiled=True
    ).astype(jnp.float32)
    outer_delta = pseudo_sum / island_count
    new_momentum = nesterov_coef * momentum + outer_delta
    new_weights = weights - outer_rate * (outer_delta + nesterov_coef * new_momentum)
    return (new_weights, new_momentum)


def solution(mesh):
    in_specs = (
        P(None, "fsdp", "isl"),
        P(None, "fsdp", "isl"),
        P("isl", None, "fsdp", None),
        P("isl", None, "fsdp", None),
        P(None, ("isl", "fsdp"), None),
        P(None, ("isl", "fsdp"), None),
        P("isl", "fsdp"),
    )
    out_specs = (P(None, "fsdp", "isl"), P(None, "fsdp", "isl"))
    return jax.shard_map(body, mesh=mesh, in_specs=in_specs, out_specs=out_specs, check_vma=False)
```

profile of v0, /device:TPU:0, one launch (start us, length us, event | category | flops | bytes accessed | tf_op | source)
XLA Modules:
  0.0 742.3 jit_solution(11448061210267699757)
XLA Ops:
  7.2 7.5 %convert_element_type.72 = bf16[3,896,1024]{2,1,0:T(8,128)(2,1)} convert(f32[3,896,1024]{2,1,0:T(8,128)} %param.7) | non-fusion elementwise | flops 2752512 | bytes 16515072 | tf_op jit(solution)/shard_map/convert_element_type | solution.py:37
  14.8 33.0 %all-gather = bf16[1,64,4096]{2,1,0:T(8,128)(2,1)S(1)} all-gather(bf16[1,8,4096]{2,1,0:T(8,128)(2,1)S(1)} %get-tuple-element.7), channel_id=2, replica_groups=mesh['isl'=4,'fsdp'=8] {'fsdp'}, dimensions={1}, use_global_device_ids=true | all-gather | bytes 589824 | tf_op jit(solution)/shard_map/all_gather | solution.py:49
  47.9 107.2 %all-gather.4.cloned.1.call-done = bf16[3,896,4096]{2,1,0:T(8,128)(2,1)} async-done(((bf16[3,896,1024]{2,1,0:T(8,128)(2,1)}), bf16[3,896,4096]{2,1,0:T(8,128)(2,1)}) %all-gather.4.cloned.1.call-update) | async-done | bytes 22020112 | tf_op jit(solution)/shard_map/all_gather | solution.py:37
  160.5 5.4 multiply_convert_fusion.5
  165.9 5.5 fusion.19
  172.1 13.0 %all-reduce = (s32[]{:T(128)}, s32[]{:T(128)}) all-reduce(s32[]{:T(128)} %bitcast.1, s32[]{:T(128)} %bitcast), channel_id=1, replica_groups=mesh['isl'=4,'fsdp'=8] {'fsdp'}, use_global_device_ids=true, to_apply=%region_1.0 | all-reduce | flops 2 | bytes 16 | tf_op jit(solution)/shard_map/psum | solution.py:68
  185.8 31.7 %all-gather.1 = bf16[1,64,4096]{2,1,0:T(8,128)(2,1)S(1)} all-gather(bf16[1,8,4096]{2,1,0:T(8,128)(2,1)S(1)} %get-tuple-element.6), channel_id=3, replica_groups=mesh['isl'=4,'fsdp'=8] {'fsdp'}, dimensions={1}, use_global_device_ids=true | all-gather | bytes 589824 | tf_op jit(solution)/shard_map/all_gather | solution.py:49
  217.4 18.9 %reduce-scatter.4.cloned.1.call-done = f32[8,4096]{1,0:T(8,128)} async-done(((f32[64,4096]{1,0:T(8,128)}), f32[8,4096]{1,0:T(8,128)}) %reduce-scatter.4.cloned.1.call-update) | async-done | bytes 131088 | tf_op jit(solution)/shard_map/reduce_scatter | solution.py:55
  237.3 31.7 %all_gather.17 = bf16[64,4096]{1,0:T(8,128)(2,1)S(1)} all-gather(bf16[8,4096]{1,0:T(8,128)(2,1)S(1)} %fusion.43), channel_id=1, replica_groups=mesh['isl'=4,'fsdp'=8] {'fsdp'}, dimensions={0}, use_global_device_ids=true | all-gather | bytes 589824 | tf_op jit(solution)/shard_map/all_gather | solution.py:60
  271.1 10.6 %fusion.23 = f32[64,896]{1,0:T(8,128)S(1)} fusion(bf16[64,4096]{1,0:T(8,128)(2,1)S(1)} %all_gather.17, bf16[3,896,4096]{2,1,0:T(8,128)(2,1)} %all-gather.4.cloned.1.call-done), kind=kOutput, calls=%fused_computation.51 | convolution fusion | flops 469819392 | bytes 8093696 | tf_op jit(solution)/shard_map/dot_general | solution.py:24
  281.7 7.2 multiply_bitcast_fusion.4
  288.9 7.3 multiply_bitcast_fusion.5
  296.2 47.5 %fusion.52 = bf16[3,896,4096]{2,1,0:T(8,128)(2,1)} fusion(bf16[1,3,896,4096]{3,2,1,0:T(8,128)(2,1)} %param.10, f32[1,896,4096]{2,1,0:T(8,128)S(1)} %multiply_bitcast_fusion.3, f32[1,896,4096]{2,1,0:T(8,128)} %multiply_bitcast_fusion.4, f32[1,896,4096]{2,1,0:T(8,128)} %multiply_bitcast_fusion.5, bf16[1,3,896,4096]{3,2,1,0:T(8,128)(2,1)} %param.9, ...), kind=kLoop, calls=%fused_computation.90 | loop fusion | flops 220200960 | bytes 132120576 | tf_op jit(solution)/shard_map/convert_element_type | solution.py:46
  349.2 5.4 multiply_convert_fusion.2
  354.7 5.5 fusion.21
  360.7 62.5 %reduce-scatter.6.cloned.1.call-done = f32[8,4096]{1,0:T(8,128)} async-done(((f32[64,4096]{1,0:T(8,128)}), f32[8,4096]{1,0:T(8,128)}) %reduce-scatter.6.cloned.1.call-update) | async-done | bytes 131088 | tf_op jit(solution)/shard_map/reduce_scatter | solution.py:55
  424.2 31.7 %all_gather.19 = bf16[64,4096]{1,0:T(8,128)(2,1)S(1)} all-gather(bf16[8,4096]{1,0:T(8,128)(2,1)S(1)} %fusion.41), channel_id=1, replica_groups=mesh['isl'=4,'fsdp'=8] {'fsdp'}, dimensions={0}, use_global_device_ids=true | all-gather | bytes 589824 | tf_op jit(solution)/shard_map/all_gather | solution.py:60
  455.9 5.4 fusion.22
  461.3 7.3 multiply_bitcast_fusion
  468.6 7.2 multiply_bitcast_fusion.1
  475.8 7.3 multiply_bitcast_fusion.2
  483.1 77.6 %fusion.13 = bf16[3,896,4096]{2,1,0:T(8,128)(2,1)} fusion(bf16[3,896,4096]{2,1,0:T(8,128)(2,1)} %all-gather.4.cloned.1.call-done, f32[1,896,4096]{2,1,0:T(8,128)} %multiply_bitcast_fusion, f32[1,896,4096]{2,1,0:T(8,128)} %multiply_bitcast_fusion.1, f32[1,896,4096]{2,1,0:T(8,128)} %multiply_bitcast_fusion.2, f32[1,896,4096]{2,1,0:T(8,128)} %copy-done, ...), kind=kLoop, calls=%fused_computation.24 | loop fusion | flops 429391872 | bytes 176160768 | tf_op jit(solution)/shard_map/convert_element_type | solution.py:80
  560.7 155.7 %reduce-scatter.8.cloned.1.call-done = bf16[3,896,1024]{2,1,0:T(8,128)(2,1)} async-done(((bf16[3,896,4096]{2,1,0:T(8,128)(2,1)}), bf16[3,896,1024]{2,1,0:T(8,128)(2,1)}) %reduce-scatter.8.cloned.1.call-update) | async-done | bytes 5505040 | tf_op jit(solution)/shard_map/reduce_scatter | solution.py:79
  716.4 19.4 %multiply_subtract_fusion = (f32[3,896,1024]{2,1,0:T(8,128)}, f32[3,896,1024]{2,1,0:T(8,128)}) fusion(f32[3,896,1024]{2,1,0:T(8,128)} %param.7, bf16[3,896,1024]{2,1,0:T(8,128)(2,1)} %reduce-scatter.8.cloned.1.call-done, f32[3,896,1024]{2,1,0:T(8,128)} %param.8), kind=kLoop, calls=%fused_computation.33 | loop fusion | flops 22020096 | bytes 49545216 | tf_op jit(solution)/shard_map/sub | solution.py:84
  (20 shorter events, 15.1 us)
Async XLA Ops:
  7.2 7.7 %copy-start.1 = (bf16[2,8,4096]{2,1,0:T(8,128)(2,1)S(1)}, bf16[2,8,4096]{2,1,0:T(8,128)(2,1)}, u32[]{:S(2)}) copy-start(bf16[2,8,4096]{2,1,0:T(8,128)(2,1)} %param.11) | copy-start | bytes 393220
  7.2 229.2 %copy-start.2 = (bf16[2,8,4096]{2,1,0:T(8,128)(2,1)S(1)}, bf16[2,8,4096]{2,1,0:T(8,128)(2,1)}, u32[]{:S(2)}) copy-start(bf16[2,8,4096]{2,1,0:T(8,128)(2,1)} %param.12) | copy-start | bytes 393220
  7.2 147.8 %all-gather.4.cloned.1.call-start = ((), (), s32[]{:S(2)}) async-start(), calls=%async_computation.3 | async-start | bytes 27525120 | tf_op jit(solution)/shard_map/all_gather | solution.py:37
  14.8 221.6 %reduce-scatter.4.cloned.1.call-start = ((), (), s32[]{:S(2)}) async-start(), calls=%async_computation.4 | async-start | bytes 1179648 | tf_op jit(solution)/shard_map/reduce_scatter | solution.py:55
  171.4 251.8 %reduce-scatter.6.cloned.1.call-start = ((), (), s32[]{:S(2)}) async-start(), calls=%async_computation.5 | async-start | bytes 1179648 | tf_op jit(solution)/shard_map/reduce_scatter | solution.py:55
  271.0 72.7 %copy-start = (f32[1,896,4096]{2,1,0:T(8,128)}, f32[1,896,4096]{2,1,0:T(8,128)S(1)}, u32[]{:S(2)}) copy-start(f32[1,896,4096]{2,1,0:T(8,128)S(1)} %multiply_bitcast_fusion.3) | copy-start | bytes 44040196
  360.1 356.3 %reduce-scatter.8.cloned.1.call-start = ((), (), s32[]{:S(2)}) async-start(), calls=%async_computation.6 | async-start | bytes 27525120 | tf_op jit(solution)/shard_map/reduce_scatter | solution.py:79
Sparse Core Ops, SparseCore 0:
  14.9 140.0 all-gather.3
  171.5 64.7 reduce-scatter.3
  360.3 62.9 reduce-scatter.5
  560.8 155.5 reduce-scatter.7
where the time goes:
time: 743 us; the launch traced here: 742 us
  waiting for transfers between devices  344 us (46%)
  other arithmetic  154 us (21%)
  blocking collectives  141 us (19%)
  matrix products  87.2 us (12%)
  between operations  15.7 us (2%)
    reduce_scatter x1, waiting for transfers between devices, body(): lax.psum_scatter(pseudo_term.astype(jnp.bfloat16), 'isl', scatter_dimensi...  156 us
    all_gather x1, waiting for transfers between devices, body(): lax.all_gather(weights.astype(jnp.bfloat16), 'isl', axis=2, tiled=True)  107 us
    reduce_scatter x2, waiting for transfers between devices, body(): lax.psum_scatter(partial_value, 'fsdp', scatter_dimension=0, tiled=True)  81.4 us
    convert_element_type x1, other arithmetic, body(): pseudo_term.astype(jnp.bfloat16)  77.6 us
    all_gather x2, blocking collectives, body(): every_input = lax.all_gather(local_inputs, 'fsdp', axis=0, tiled=True)  64.7 us
    all_gather x2, blocking collectives, body(): slopes = lax.all_gather(own_slopes, 'fsdp', axis=0, tiled=True)  63.4 us
    convert_element_type x1, other arithmetic, body(): rounded = current.astype(jnp.bfloat16)  47.5 us
    dot_general x6, matrix products, contract_first(): lax.dot_general(left_side, right_side, (((0,), (0,)), ((), ())), preferre...  38.4 us
  transfers between devices with their start and end apart: 4, of which 4 were waited for; matrix products, arithmetic and copies ran while one was open for 0% of the time, Pallas kernels for 0%

commit v1 on v0

--- a/solution.py
+++ b/solution.py
@@ -3,6 +3,7 @@
 import jax.numpy as jnp
 from jax import lax
 from jax.sharding import PartitionSpec as P
+from jax.lax import all_gather
 
 D = 4096
 FF = 7168
@@ -34,7 +35,7 @@
 
 def body(weights, momentum, first_moment, second_moment, inputs, targets, overflow_step):
     island_count = lax.axis_size("isl")
-    gathered = lax.all_gather(weights.astype(jnp.bfloat16), "isl", axis=2, tiled=True).astype(
+    gathered = jnp.concatenate(all_gather(weights.astype(jnp.bfloat16), "isl"), 2).astype(
         weights.dtype
     )
     current = gathered

time: 743 us -> 859 us (1.16)
  local copies, waits for them, and re-layouts: 0.02 us -> 103 us
  other arithmetic: 154 us -> 189 us
  waiting for transfers between devices: 344 us -> 325 us
    convert_element_type x0 -> x1, local copies, waits for them, and re-layouts: none -> 51.9 us  [body(): jnp.concatenate(all_gather(weights.astype(jnp.bfloat16), 'isl'), 2)]
    unnamed x6 -> x11, local copies, waits for them, and re-layouts: 0.01 us -> 32.6 us
    reshape x0 -> x1, other arithmetic: none -> 30.7 us  [body(): jnp.concatenate(all_gather(weights.astype(jnp.bfloat16), 'isl'), 2)]
    reduce_scatter x2, waiting for transfers between devices: 81.4 us -> 61.8 us  [body(): lax.psum_scatter(partial_value, 'fsdp', scatter_dimension=0, tiled=True)]
    slice x0 -> x1, local copies, waits for them, and re-layouts: none -> 18.8 us  [body(): rounded[2]]
  transfers between devices with their start and end apart: 4 -> 4, of which waited for: 4 -> 3; matrix products, arithmetic and copies ran while one was open for 0% -> 6% of each run, Pallas kernels for 0% -> 0%
where the time goes in v1:
time: 859 us; the launch traced here: 854 us
  waiting for transfers between devices  325 us (38%)
  other arithmetic  189 us (22%)
  blocking collectives  141 us (16%)
  local copies, waits for them, and re-layouts  103 us (12%)
  matrix products  79.5 us (9%)
  between operations  16.1 us (2%)
    reduce_scatter x1, waiting for transfers between devices, body(): lax.psum_scatter(pseudo_term.astype(jnp.bfloat16), 'isl', scatter_dimensi...  156 us
    all_gather x1, waiting for transfers between devices, body(): all_gather(weights.astype(jnp.bfloat16), 'isl')  107 us
    convert_element_type x1, other arithmetic, body(): pseudo_term.astype(jnp.bfloat16)  76.8 us
    all_gather x2, blocking collectives, body(): every_input = lax.all_gather(local_inputs, 'fsdp', axis=0, tiled=True)  64.6 us
    all_gather x2, blocking collectives, body(): slopes = lax.all_gather(own_slopes, 'fsdp', axis=0, tiled=True)  63.3 us
    reduce_scatter x2, waiting for transfers between devices, body(): lax.psum_scatter(partial_value, 'fsdp', scatter_dimension=0, tiled=True)  61.8 us
    convert_element_type x1, other arithmetic, body(): rounded = current.astype(jnp.bfloat16)  52.6 us
    convert_element_type x1, local copies, waits for them, and re-layouts, body(): jnp.concatenate(all_gather(weights.astype(jnp.bfloat16), 'isl'), 2)  51.9 us
  transfers between devices with their start and end apart: 4, of which 3 were waited for; matrix products, arithmetic and copies ran while one was open for 6% of the time, Pallas kernels for 0%

profile of v1, /device:TPU:0, one launch (start us, length us, event | category | flops | bytes accessed | tf_op | source)
XLA Modules:
  0.0 853.5 jit_solution(12643583377808924011)
XLA Ops:
  7.2 7.5 convert_element_type.75
  14.8 33.0 %all-gather.1 = bf16[1,64,4096]{2,1,0:T(8,128)(2,1)S(1)} all-gather(bf16[1,8,4096]{2,1,0:T(8,128)(2,1)S(1)} %get-tuple-element.12), channel_id=3, replica_groups=mesh['isl'=4,'fsdp'=8] {'fsdp'}, dimensions={1}, use_global_device_ids=true | all-gather | bytes 589824 | tf_op jit(solution)/shard_map/all_gather | solution.py:50
  47.8 107.2 %all-gather.5.cloned.1.call-done = bf16[12,896,1024]{2,1,0:T(8,128)(2,1)} async-done(((bf16[3,896,1024]{2,1,0:T(8,128)(2,1)}), bf16[12,896,1024]{2,1,0:T(8,128)(2,1)}) %all-gather.5.cloned.1.call-update) | async-done | bytes 22020112 | tf_op jit(solution)/shard_map/all_gather | solution.py:38
  155.0 30.7 %copy_bitcast_fusion = (bf16[3,896,4,1024]{3,2,1,0:T(4,128)(2,1)}, f32[3,896,4,1024]{3,2,1,0:T(4,128)}) fusion(bf16[4,3,896,1024]{3,2,1,0:T(8,128)(2,1)} %bitcast.123), kind=kLoop, calls=%fused_computation.23 | loop fusion | flops 11010048 | bytes 88080384 | tf_op jit(solution)/shard_map/reshape | solution.py:38
  185.7 18.8 %fusion.46 = (bf16[1,896,4,1024]{3,2,1,0:T(4,128)(2,1)}, bf16[1,896,4,1024]{3,2,1,0:T(4,128)(2,1)}, bf16[1,896,4,1024]{3,2,1,0:T(4,128)(2,1)}) fusion(bf16[3,896,4,1024]{3,2,1,0:T(4,128)(2,1)} %get-tuple-element.9), kind=kLoop, calls=%fused_computation.82 | loop fusion | bytes 44040192 | tf_op jit(solution)/shard_map/slice | solution.py:55
  204.5 7.9 copy.13
  212.4 13.5 %copy.12 = bf16[112,8,4,1024]{3,1,2,0:T(8,128)(2,1)} copy(bf16[112,8,4,1024]{3,2,1,0:T(4,128)(2,1)} %bitcast.121) | data formatting | bytes 14680064
  225.9 11.1 %copy.11 = bf16[112,8,4,1024]{3,1,2,0:T(8,128)(2,1)} copy(bf16[112,8,4,1024]{3,2,1,0:T(4,128)(2,1)} %bitcast.120) | data formatting | bytes 14680064
  251.0 13.1 %all-reduce = (s32[]{:T(128)}, s32[]{:T(128)}) all-reduce(s32[]{:T(128)} %bitcast.3, s32[]{:T(128)} %bitcast.2), channel_id=1, replica_groups=mesh['isl'=4,'fsdp'=8] {'fsdp'}, use_global_device_ids=true, to_apply=%region_1.0 | all-reduce | flops 2 | bytes 16 | tf_op jit(solution)/shard_map/psum | solution.py:69
  264.8 31.6 %all-gather.2 = bf16[1,64,4096]{2,1,0:T(8,128)(2,1)S(1)} all-gather(bf16[1,8,4096]{2,1,0:T(8,128)(2,1)S(1)} %get-tuple-element.11), channel_id=4, replica_groups=mesh['isl'=4,'fsdp'=8] {'fsdp'}, dimensions={1}, use_global_device_ids=true | all-gather | bytes 589824 | tf_op jit(solution)/shard_map/all_gather | solution.py:50
  296.3 51.9 %reshape.29 = f32[3,896,4096]{2,1,0:T(8,128)} reshape(f32[3,896,4,1024]{3,2,1,0:T(4,128)} %get-tuple-element.10) | data formatting | bytes 88080384 | tf_op jit(solution)/shard_map/convert_element_type | solution.py:38
  349.2 31.6 %all_gather.21 = bf16[64,4096]{1,0:T(8,128)(2,1)S(1)} all-gather(bf16[8,4096]{1,0:T(8,128)(2,1)S(1)} %fusion.35), channel_id=1, replica_groups=mesh['isl'=4,'fsdp'=8] {'fsdp'}, dimensions={0}, use_global_device_ids=true | all-gather | bytes 589824 | tf_op jit(solution)/shard_map/all_gather | solution.py:61
  388.4 7.9 multiply_bitcast_fusion.4
  396.3 7.3 multiply_bitcast_fusion.5
  403.6 52.6 %fusion.45 = bf16[3,896,4096]{2,1,0:T(8,128)(2,1)} fusion(f32[3,896,4096]{2,1,0:T(8,128)} %reshape.29, bf16[1,3,896,4096]{3,2,1,0:T(8,128)(2,1)} %param.10, f32[1,896,4096]{2,1,0:T(8,128)S(1)} %multiply_bitcast_fusion.3, f32[1,896,4096]{2,1,0:T(8,128)} %multiply_bitcast_fusion.4, f32[1,896,4096]{2,1,0:T(8,128)} %multiply_bitcast_fusion.5, ...), kind=kLoop, calls=%fused_computation.81 | loop fusion | flops 209190912 | bytes 154140672 | tf_op jit(solution)/shard_map/convert_element_type | solution.py:47
  467.1 5.5 fusion.16
  473.3 61.8 %reduce-scatter.6.cloned.1.call-done = f32[8,4096]{1,0:T(8,128)} async-done(((f32[64,4096]{1,0:T(8,128)}), f32[8,4096]{1,0:T(8,128)}) %reduce-scatter.6.cloned.1.call-update) | async-done | bytes 131088 | tf_op jit(solution)/shard_map/reduce_scatter | solution.py:56
  536.0 31.7 %all_gather.23 = bf16[64,4096]{1,0:T(8,128)(2,1)S(1)} all-gather(bf16[8,4096]{1,0:T(8,128)(2,1)S(1)} %fusion.33), channel_id=1, replica_groups=mesh['isl'=4,'fsdp'=8] {'fsdp'}, dimensions={0}, use_global_device_ids=true | all-gather | bytes 589824 | tf_op jit(solution)/shard_map/all_gather | solution.py:61
  573.2 7.2 multiply_bitcast_fusion
  580.4 7.2 multiply_bitcast_fusion.1
  587.6 7.3 multiply_bitcast_fusion.2
  594.9 76.8 %fusion.12 = bf16[3,896,4096]{2,1,0:T(8,128)(2,1)} fusion(f32[3,896,4096]{2,1,0:T(8,128)} %reshape.29, f32[1,896,4096]{2,1,0:T(8,128)} %multiply_bitcast_fusion, f32[1,896,4096]{2,1,0:T(8,128)} %multiply_bitcast_fusion.1, f32[1,896,4096]{2,1,0:T(8,128)} %multiply_bitcast_fusion.2, f32[1,896,4096]{2,1,0:T(8,128)} %copy-done, ...), kind=kLoop, calls=%fused_computation.22 | loop fusion | flops 418381824 | bytes 198180864 | tf_op jit(solution)/shard_map/convert_element_type | solution.py:81
  671.7 155.7 %reduce-scatter.8.cloned.1.call-done = bf16[3,896,1024]{2,1,0:T(8,128)(2,1)} async-done(((bf16[3,896,4096]{2,1,0:T(8,128)(2,1)}), bf16[3,896,1024]{2,1,0:T(8,128)(2,1)}) %reduce-scatter.8.cloned.1.call-update) | async-done | bytes 5505040 | tf_op jit(solution)/shard_map/reduce_scatter | solution.py:80
  827.4 19.4 %multiply_subtract_fusion = (f32[3,896,1024]{2,1,0:T(8,128)}, f32[3,896,1024]{2,1,0:T(8,128)}) fusion(f32[3,896,1024]{2,1,0:T(8,128)} %param.7, bf16[3,896,1024]{2,1,0:T(8,128)(2,1)} %reduce-scatter.8.cloned.1.call-done, f32[3,896,1024]{2,1,0:T(8,128)} %param.8), kind=kLoop, calls=%fused_computation.30 | loop fusion | flops 22020096 | bytes 49545216 | tf_op jit(solution)/shard_map/sub | solution.py:85
  (28 shorter events, 39.2 us)
Async XLA Ops:
  7.2 7.6 copy-start.2
  7.2 147.8 %all-gather.5.cloned.1.call-start = ((), (), s32[]{:S(2)}) async-start(), calls=%async_computation.6 | async-start | bytes 27525120 | tf_op jit(solution)/shard_map/all_gather | solution.py:38
  14.7 333.6 %reduce-scatter.4.cloned.1.call-start = ((), (), s32[]{:S(2)}) async-start(), calls=%async_computation.3 | async-start | bytes 1179648 | tf_op jit(solution)/shard_map/reduce_scatter | solution.py:56
  212.4 35.5 %copy-start.1 = (bf16[112,8,4,1024]{3,1,2,0:T(8,128)(2,1)}, bf16[112,8,4,1024]{3,1,2,0:T(8,128)(2,1)S(1)}, u32[]{:S(2)}) copy-start(bf16[112,8,4,1024]{3,1,2,0:T(8,128)(2,1)S(1)} %copy.13) | copy-start | bytes 22020100
  250.3 284.7 %reduce-scatter.6.cloned.1.call-start = ((), (), s32[]{:S(2)}) async-start(), calls=%async_computation.4 | async-start | bytes 1179648 | tf_op jit(solution)/shard_map/reduce_scatter | solution.py:56
  296.3 51.9 %copy-start.3 = (bf16[2,8,4096]{2,1,0:T(8,128)(2,1)S(1)}, bf16[2,8,4096]{2,1,0:T(8,128)(2,1)}, u32[]{:S(2)}) copy-start(bf16[2,8,4096]{2,1,0:T(8,128)(2,1)} %param.12) | copy-start | bytes 393220
  388.4 67.9 %copy-start = (f32[1,896,4096]{2,1,0:T(8,128)}, f32[1,896,4096]{2,1,0:T(8,128)S(1)}, u32[]{:S(2)}) copy-start(f32[1,896,4096]{2,1,0:T(8,128)S(1)} %multiply_bitcast_fusion.3) | copy-start | bytes 44040196
  472.6 354.8 %reduce-scatter.8.cloned.1.call-start = ((), (), s32[]{:S(2)}) async-start(), calls=%async_computation.5 | async-start | bytes 27525120 | tf_op jit(solution)/shard_map/reduce_scatter | solution.py:80
Sparse Core Ops, SparseCore 0:
  14.8 140.0 all-gather.4
  250.5 64.6 reduce-scatter.3
  472.7 62.3 reduce-scatter.5
  671.8 155.4 reduce-scatter.7
